TPU v7x, 32 devices: a whole 2x2x4 slice. The times are simulated.
32 devices in a mesh: shard: 2 (over x), ctx: 4 (over z), tp: 4 (over y, core).
Axes of the slice: x: 2, y: 2, z: 4, core: 2. Of those that a mesh axis runs over, the one named last changes fastest.
Arguments:
- x_img: bfloat16 [6, 1024, 1536], P('shard', ('ctx', 'tp')), may hold values from -6 to 6
- x_txt: bfloat16 [6, 160, 1536], P('shard', ('ctx', 'tp')), may hold values from -6 to 6
- cond: bfloat16 [6, 1536], P('shard'), may hold values from -6 to 6
- lengths: int32 [6], P('shard'), may hold values from 77 to 154, as said below
- mod_w: bfloat16 [2, 1536, 6, 1536], P(None, ('shard', 'ctx'), None, 'tp'), may hold values from -0.15625 to 0.15625
- qkv_w: bfloat16 [2, 3, 1536, 1536], P(None, None, ('shard', 'ctx'), 'tp'), may hold values from -0.15625 to 0.15625
- o_w: bfloat16 [2, 1536, 1536], P(None, 'tp', ('shard', 'ctx')), may hold values from -0.875 to 0.875
- up_w: bfloat16 [2, 1536, 6144], P(None, ('shard', 'ctx'), 'tp'), may hold values from -0.15625 to 0.15625
- down_w: bfloat16 [2, 6144, 1536], P(None, 'tp', ('shard', 'ctx')), may hold values from -0.078125 to 0.078125
- norm_gain: float32 [2, 2, 64], replicated, may hold values from 1 to 1.6
- threshold: float32 [], replicated, may hold values from 1 to 2
- cot_img: bfloat16 [6, 1024, 1536], P('shard', ('ctx', 'tp')), may hold values from -6 to 6
- cot_txt: bfloat16 [6, 160, 1536], P('shard', ('ctx', 'tp')), may hold values from -6 to 6
Outputs:
- out_img: bfloat16 [6, 1024, 1536], P('shard', ('ctx', 'tp'))
- out_txt: bfloat16 [6, 160, 1536], P('shard', ('ctx', 'tp'))
- grad_img: float32 [6, 1024, 1536], P('shard', ('ctx', 'tp'))
- grad_txt: float32 [6, 160, 1536], P('shard', ('ctx', 'tp'))
- grad_cond: float32 [6, 1536], P('shard')
- grad_mod: float32 [2, 1536, 6, 1536], P(None, ('shard', 'ctx'), None, 'tp')
- grad_qkv: float32 [2, 3, 1536, 1536], P(None, None, ('shard', 'ctx'), 'tp')
- grad_o: float32 [2, 1536, 1536], P(None, 'tp', ('shard', 'ctx'))
- grad_up: float32 [2, 1536, 6144], P(None, ('shard', 'ctx'), 'tp')
- grad_down: float32 [2, 6144, 1536], P(None, 'tp', ('shard', 'ctx'))
- grad_gain: float32 [2, 2, 64], replicated
- clipped_qk: float32 [2, 2, 1536, 1536], P(None, None, ('shard', 'ctx'), 'tp')
- logit_peaks: float32 [24], P('tp')
Inputs may be any that keep to these rules, and one draw needn't show every extreme that they name: lengths: text tokens of a sequence; some sequence has exactly 154.
All inputs are finite; a program needn't handle non-finite values.
Results may differ from a plain program's by a relative error of at most 0.017.
Values may be sent and summed in bfloat16 or wider, within the bound.
No kernel may reach another device: no remote copies, remote signals or barrier semaphores. Data moves between devices by JAX's collectives and lax.ppermute only.
A program may use at most 256 MiB of HBM per device.

v0:
```python
import jax
import jax.numpy as jnp
from jax import lax
from jax.sharding import PartitionSpec as P

EPS = 1e-06
QUERY_SCALE = 0.125


def layer_norm(values):
    center = values - jnp.mean(values, axis=-1, keepdims=True)
    spread = jnp.mean(center * center, axis=-1, keepdims=True)
    return center * lax.rsqrt(spread + EPS)


def modulate(values, shift, scale):
    return layer_norm(values) * (1.0 + scale) + shift


def head_norm(values, gain_vec, factor):
    shape_in = values.shape
    split_heads = values.reshape(
        shape_in[:-1] + (shape_in[-1] // gain_vec.shape[0], gain_vec.shape[0])
    )
    square = jnp.mean(split_heads * split_heads, axis=-1, keepdims=True)
    return (split_heads * lax.rsqrt(square + EPS) * gain_vec * factor).reshape(shape_in)


def gelu_tanh(values):
    return jax.nn.gelu(values, approximate=True)


def gather_rows(first, second):
    return (
        lax.all_gather(first, "tp", axis=1, tiled=True),
        lax.all_gather(second, "tp", axis=1, tiled=True),
    )


def reduce_rows(first, second):
    return (
        lax.psum_scatter(first, "tp", scatter_dimension=1, tiled=True),
        lax.psum_scatter(second, "tp", scatter_dimension=1, tiled=True),
    )


def split_heads_major(values, head_dim):
    seq_count, row_count, columns = values.shape
    return values.reshape(seq_count, row_count, columns // head_dim, head_dim).transpose(2, 0, 1, 3)


def merge_heads(values):
    head_count, seq_count, row_count, head_dim = values.shape
    return values.transpose(1, 2, 0, 3).reshape(seq_count, row_count, head_count * head_dim)


def key_mask(lengths, img_member, txt_member, ctx_count):
    member_rows = img_member + txt_member
    key_place = jnp.arange(member_rows * ctx_count, dtype=jnp.int32)
    within = key_place % member_rows
    member = key_place // member_rows
    text_place = member * txt_member + within - img_member
    return (within < img_member)[None, :] | (text_place[None, :] < lengths[:, None])


def local(
    x_img,
    x_txt,
    cond,
    lengths,
    mod_w,
    qkv_w,
    o_w,
    up_w,
    down_w,
    norm_gain,
    threshold,
    cot_img,
    cot_txt,
):
    tp_count = lax.axis_size("tp")
    ctx_count = lax.axis_size("ctx")
    shard_count = lax.axis_size("shard")
    head_dim = norm_gain.shape[2]
    img_member = x_img.shape[1] * tp_count
    txt_member = x_txt.shape[1] * tp_count
    local_feat = mod_w.shape[3]
    owned_rows = mod_w.shape[1]
    gathered = (
        lax.all_gather(qkv_w, ("shard", "ctx"), axis=2, tiled=True),
        lax.all_gather(o_w, ("shard", "ctx"), axis=2, tiled=True),
        lax.all_gather(up_w, ("shard", "ctx"), axis=1, tiled=True),
        lax.all_gather(down_w, ("shard", "ctx"), axis=2, tiled=True),
    )
    qkv_all, out_all, up_all, down_all = gathered
    cond_float = cond.astype(jnp.float32)
    cond_act = jax.nn.silu(cond_float).astype(jnp.bfloat16)
    mod_all = lax.all_gather(mod_w, ("shard", "ctx"), axis=1, tiled=True)
    mod_local = jnp.einsum("sd,tdkf->tskf", cond_act, mod_all, preferred_element_type=jnp.float32)
    modulation = lax.all_gather(mod_local, "tp", axis=3, tiled=True)
    inputs = (x_img.astype(jnp.float32), x_txt.astype(jnp.float32))

    def entry(stream, index):
        return modulation[stream, :, index][:, None, :]

    first_low = [
        modulate(inputs[s], entry(s, 0), entry(s, 1)).astype(jnp.bfloat16) for s in range(2)
    ]
    first_in = gather_rows(first_low[0], first_low[1])
    projected = [
        jnp.einsum("srd,cdf->csrf", first_in[s], qkv_all[s], preferred_element_type=jnp.float32)
        for s in range(2)
    ]
    queries = jnp.concatenate(
        [head_norm(projected[s][0], norm_gain[s, 0], QUERY_SCALE) for s in range(2)], axis=1
    ).astype(jnp.bfloat16)
    keys_local = jnp.concatenate(
        [head_norm(projected[s][1], norm_gain[s, 1], 1.0) for s in range(2)], axis=1
    ).astype(jnp.bfloat16)
    values_local = jnp.concatenate([projected[s][2] for s in range(2)], axis=1).astype(jnp.bfloat16)
    keys_all, values_all = (
        lax.all_gather(keys_local, "ctx", axis=1, tiled=True),
        lax.all_gather(values_local, "ctx", axis=1, tiled=True),
    )
    key_masks = key_mask(lengths, img_member, txt_member, ctx_count)

    def attend_head(operands):
        query_head, key_head, value_head = operands
        scores = jnp.einsum(
            "sqd,skd->sqk", query_head, key_head, preferred_element_type=jnp.float32
        )
        masked = jnp.where(key_masks[:, None, :], scores, -jnp.inf)
        highest = jnp.max(masked, axis=-1, keepdims=True)
        weights_exp = jnp.exp(masked - highest)
        denominator = jnp.sum(weights_exp, axis=-1, keepdims=True)
        probabilities = (weights_exp / denominator).astype(jnp.bfloat16)
        mixed_out = jnp.einsum(
            "sqk,skd->sqd", probabilities, value_head, preferred_element_type=jnp.float32
        )
        return (
            mixed_out.astype(jnp.bfloat16),
            (highest + jnp.log(denominator))[..., 0],
            jnp.max(highest),
        )

    query_heads = split_heads_major(queries, head_dim)
    key_heads = split_heads_major(keys_all, head_dim)
    value_heads = split_heads_major(values_all, head_dim)
    attended, log_norm, head_peaks = lax.map(attend_head, (query_heads, key_heads, value_heads))
    peaks = lax.pmax(head_peaks, ("shard", "ctx"))
    attended = merge_heads(attended)
    segments = (attended[:, :img_member], attended[:, img_member:])
    attn_parts = [
        jnp.einsum("srf,fd->srd", segments[s], out_all[s], preferred_element_type=jnp.float32)
        for s in range(2)
    ]
    attn_out = reduce_rows(attn_parts[0], attn_parts[1])
    mid = [inputs[s] + entry(s, 2) * attn_out[s] for s in range(2)]
    second_low = [modulate(mid[s], entry(s, 3), entry(s, 4)).astype(jnp.bfloat16) for s in range(2)]
    second_in = gather_rows(second_low[0], second_low[1])
    hidden_pre = [
        jnp.einsum("srd,df->srf", second_in[s], up_all[s], preferred_element_type=jnp.float32)
        for s in range(2)
    ]
    hidden_low = [gelu_tanh(hidden_pre[s]).astype(jnp.bfloat16) for s in range(2)]
    mlp_parts = [
        jnp.einsum("srf,fd->srd", hidden_low[s], down_all[s], preferred_element_type=jnp.float32)
        for s in range(2)
    ]
    mlp_out = reduce_rows(mlp_parts[0], mlp_parts[1])
    results = [(mid[s] + entry(s, 5) * mlp_out[s]).astype(jnp.bfloat16) for s in range(2)]
    qkv_back, out_back, up_back, down_back = (
        lax.all_gather(qkv_w, ("shard", "ctx"), axis=2, tiled=True),
        lax.all_gather(o_w, ("shard", "ctx"), axis=2, tiled=True),
        lax.all_gather(up_w, ("shard", "ctx"), axis=1, tiled=True),
        lax.all_gather(down_w, ("shard", "ctx"), axis=2, tiled=True),
    )
    grad_out = (cot_img.astype(jnp.float32), cot_txt.astype(jnp.float32))
    mlp_grad_low = [(grad_out[s] * entry(s, 5)).astype(jnp.bfloat16) for s in range(2)]
    gate_two = [jnp.sum(grad_out[s] * mlp_out[s], axis=1) for s in range(2)]
    mlp_grad_in = gather_rows(mlp_grad_low[0], mlp_grad_low[1])
    grad_down = jnp.stack(
        [
            jnp.einsum(
                "srf,srd->fd", hidden_low[s], mlp_grad_in[s], preferred_element_type=jnp.float32
            )
            for s in range(2)
        ]
    )
    pre_grad = []
    for s in range(2):
        hidden_back = jnp.einsum(
            "srd,fd->srf", mlp_grad_in[s], down_back[s], preferred_element_type=jnp.float32
        )
        unused, gelu_vjp = jax.vjp(gelu_tanh, hidden_pre[s])
        pre_grad.append(gelu_vjp(hidden_back)[0].astype(jnp.bfloat16))
    grad_up = jnp.stack(
        [
            jnp.einsum("srd,srf->df", second_in[s], pre_grad[s], preferred_element_type=jnp.float32)
            for s in range(2)
        ]
    )
    second_parts = [
        jnp.einsum("srf,df->srd", pre_grad[s], up_back[s], preferred_element_type=jnp.float32)
        for s in range(2)
    ]
    second_grad = reduce_rows(second_parts[0], second_parts[1])
    mid_grad = []
    shift_two = []
    scale_two = []
    for s in range(2):
        unused, mod_vjp = jax.vjp(modulate, mid[s], entry(s, 3), entry(s, 4))
        mid_part, shift_part, scale_part = mod_vjp(second_grad[s])
        mid_grad.append(grad_out[s] + mid_part)
        shift_two.append(shift_part[:, 0])
        scale_two.append(scale_part[:, 0])
    attn_grad_low = [(mid_grad[s] * entry(s, 2)).astype(jnp.bfloat16) for s in range(2)]
    gate_one = [jnp.sum(mid_grad[s] * attn_out[s], axis=1) for s in range(2)]
    attn_grad_in = gather_rows(attn_grad_low[0], attn_grad_low[1])
    grad_outproj = jnp.stack(
        [
            jnp.einsum(
                "srf,srd->fd", segments[s], attn_grad_in[s], preferred_element_type=jnp.float32
            )
            for s in range(2)
        ]
    )
    mixed_grad = jnp.concatenate(
        [
            jnp.einsum(
                "srd,fd->srf", attn_grad_in[s], out_back[s], preferred_element_type=jnp.float32
            )
            for s in range(2)
        ],
        axis=1,
    ).astype(jnp.bfloat16)

    def attend_back(operands):
        query_head, key_head, value_head, grad_head, log_head = operands
        scores = jnp.einsum(
            "sqd,skd->sqk", query_head, key_head, preferred_element_type=jnp.float32
        )
        masked = jnp.where(key_masks[:, None, :], scores, -jnp.inf)
        probabilities = jnp.exp(masked - log_head[..., None])
        grad_prob = jnp.einsum(
            "sqd,skd->sqk", grad_head, value_head, preferred_element_type=jnp.float32
        )
        grad_score = (
            probabilities * (grad_prob - jnp.sum(probabilities * grad_prob, axis=-1, keepdims=True))
        ).astype(jnp.bfloat16)
        grad_query = jnp.einsum(
            "sqk,skd->sqd", grad_score, key_head, preferred_element_type=jnp.float32
        )
        grad_key = jnp.einsum(
            "sqk,sqd->skd", grad_score, query_head, preferred_element_type=jnp.float32
        )
        grad_value = jnp.einsum(
            "sqk,sqd->skd",
            probabilities.astype(jnp.bfloat16),
            grad_head,
            preferred_element_type=jnp.float32,
        )
        return (grad_query, grad_key, grad_value)

    query_grads, key_grads, value_grads = lax.map(
        attend_back,
        (query_heads, key_heads, value_heads, split_heads_major(mixed_grad, head_dim), log_norm),
    )
    key_sum, value_sum = (
        lax.psum_scatter(
            merge_heads(key_grads).astype(jnp.bfloat16), "ctx", scatter_dimension=1, tiled=True
        ).astype(jnp.float32),
        lax.psum_scatter(
            merge_heads(value_grads).astype(jnp.bfloat16), "ctx", scatter_dimension=1, tiled=True
        ).astype(jnp.float32),
    )
    query_sum = merge_heads(query_grads)
    bounds = ((0, img_member), (img_member, img_member + txt_member))
    grad_qkv_parts = []
    first_parts = []
    gain_terms = []
    for s in range(2):
        start_row, stop_row = bounds[s]
        unused, query_vjp = jax.vjp(
            lambda v, g: head_norm(v, g, QUERY_SCALE), projected[s][0], norm_gain[s, 0]
        )
        query_raw_grad, query_gain_grad = query_vjp(query_sum[:, start_row:stop_row])
        unused, key_vjp = jax.vjp(
            lambda v, g: head_norm(v, g, 1.0), projected[s][1], norm_gain[s, 1]
        )
        key_raw_grad, key_gain_grad = key_vjp(key_sum[:, start_row:stop_row])
        proj_grad = jnp.stack(
            [query_raw_grad, key_raw_grad, value_sum[:, start_row:stop_row]]
        ).astype(jnp.bfloat16)
        grad_qkv_parts.append(
            jnp.einsum("srd,csrf->cdf", first_in[s], proj_grad, preferred_element_type=jnp.float32)
        )
        first_parts.append(
            jnp.einsum("csrf,cdf->srd", proj_grad, qkv_back[s], preferred_element_type=jnp.float32)
        )
        gain_terms.append(jnp.stack([query_gain_grad, key_gain_grad]))
    first_grad = reduce_rows(first_parts[0], first_parts[1])
    input_grads = []
    mod_terms = []
    for s in range(2):
        unused, mod_vjp = jax.vjp(modulate, inputs[s], entry(s, 0), entry(s, 1))
        input_part, shift_part, scale_part = mod_vjp(first_grad[s])
        input_grads.append(mid_grad[s] + input_part)
        mod_terms.append(
            jnp.stack(
                [
                    shift_part[:, 0],
                    scale_part[:, 0],
                    gate_one[s],
                    shift_two[s],
                    scale_two[s],
                    gate_two[s],
                ],
                axis=1,
            )
        )
    mod_grad = lax.psum(jnp.stack(mod_terms).astype(jnp.bfloat16), ("ctx", "tp")).astype(
        jnp.float32
    )
    gain_grad = lax.psum(jnp.stack(gain_terms), ("shard", "ctx", "tp"))
    own_mod = lax.dynamic_slice_in_dim(
        mod_grad, lax.axis_index("tp") * local_feat, local_feat, axis=3
    ).astype(jnp.bfloat16)
    seq_count = cond_act.shape[0]
    cond_blocks = cond_act.reshape(seq_count, shard_count, ctx_count, owned_rows)
    cond_member = lax.dynamic_index_in_dim(
        cond_blocks, lax.axis_index("ctx"), axis=2, keepdims=False
    ).reshape(seq_count, shard_count * owned_rows)
    grad_mod_terms = jnp.einsum(
        "sd,tskf->tdkf", cond_member, own_mod, preferred_element_type=jnp.float32
    )
    grad_mod = lax.psum_scatter(
        grad_mod_terms.astype(jnp.bfloat16), "shard", scatter_dimension=1, tiled=True
    ).astype(jnp.float32)
    cond_part = jnp.einsum("tskf,tdkf->sd", own_mod, mod_all, preferred_element_type=jnp.float32)
    cond_total = lax.psum(cond_part, "tp")
    unused, silu_vjp = jax.vjp(jax.nn.silu, cond_float)
    grad_cond = silu_vjp(cond_total)[0]
    owned_grads = (
        lax.psum_scatter(
            jnp.stack(grad_qkv_parts), ("shard", "ctx"), scatter_dimension=2, tiled=True
        ),
        lax.psum_scatter(grad_outproj, ("shard", "ctx"), scatter_dimension=2, tiled=True),
        lax.psum_scatter(grad_up, ("shard", "ctx"), scatter_dimension=1, tiled=True),
        lax.psum_scatter(grad_down, ("shard", "ctx"), scatter_dimension=2, tiled=True),
    )
    factor = jnp.sqrt(threshold / jnp.maximum(peaks, threshold))
    columns = jnp.repeat(factor, head_dim)
    clipped = qkv_w[:, :2].astype(jnp.float32) * columns
    return (
        results[0],
        results[1],
        input_grads[0],
        input_grads[1],
        grad_cond,
        grad_mod,
        owned_grads[0],
        owned_grads[1],
        owned_grads[2],
        owned_grads[3],
        gain_grad,
        clipped,
        peaks,
    )


def solution(mesh):
    return jax.shard_map(
        local,
        mesh=mesh,
        in_specs=(
            P("shard", ("ctx", "tp"), None),
            P("shard", ("ctx", "tp"), None),
            P("shard", None),
            P("shard"),
            P(None, ("shard", "ctx"), None, "tp"),
            P(None, None, ("shard", "ctx"), "tp"),
            P(None, "tp", ("shard", "ctx")),
            P(None, ("shard", "ctx"), "tp"),
            P(None, "tp", ("shard", "ctx")),
            P(),
            P(),
            P("shard", ("ctx", "tp"), None),
            P("shard", ("ctx", "tp"), None),
        ),
        out_specs=(
            P("shard", ("ctx", "tp"), None),
            P("shard", ("ctx", "tp"), None),
            P("shard", ("ctx", "tp"), None),
            P("shard", ("ctx", "tp"), None),
            P("shard", None),
            P(None, ("shard", "ctx"), None, "tp"),
            P(None, None, ("shard", "ctx"), "tp"),
            P(None, "tp", ("shard", "ctx")),
            P(None, ("shard", "ctx"), "tp"),
            P(None, "tp", ("shard", "ctx")),
            P(),
            P(None, None, ("shard", "ctx"), "tp"),
            P("tp"),
        ),
        check_vma=False,
    )
```

profile of v0, /device:TPU:0, one launch (start us, length us, event | category | flops | bytes accessed | tf_op | source)
XLA Modules:
  0.0 3243.1 jit_solution(17155912777045053228)
XLA Ops:
  9.2 199.0 %all-gather.12.cloned.1.call-done = bf16[2,1536,6,384]{3,1,2,0:T(8,128)(2,1)} async-done(((bf16[2,192,6,384]{3,1,2,0:T(8,128)(2,1)}), bf16[2,1536,6,384]{3,1,2,0:T(8,128)(2,1)}) %all-gather.12.cloned.1.call-update) | async-done | bytes 14155792 | tf_op jit(solution)/shard_map/all_gather | solution.py:98
  208.2 6.9 convolution_bitcast_fusion.12
  226.2 7.1 all_gather.56
  233.3 83.5 %all-gather.16.cloned.1.call-done = bf16[2,3,1536,384]{3,2,1,0:T(8,128)(2,1)} async-done(((bf16[2,3,192,384]{3,2,1,0:T(8,128)(2,1)}), bf16[2,3,1536,384]{3,2,1,0:T(8,128)(2,1)}) %all-gather.16.cloned.1.call-update) | async-done | bytes 7077904 | tf_op jit(solution)/shard_map/all_gather | solution.py:90
  321.9 19.3 all-gather.14.cloned.1.call-done
  356.7 38.9 %all-gather.22.cloned.1.call-done = bf16[2,384,1536]{1,0,2:T(2,128)(2,1)} async-done(((bf16[2,384,192]{1,0,2:T(2,128)(2,1)}), bf16[2,384,1536]{1,0,2:T(2,128)(2,1)}) %all-gather.22.cloned.1.call-update) | async-done | bytes 2359312 | tf_op jit(solution)/shard_map/all_gather | solution.py:91
  395.6 7.2 fusion.192
  412.6 40.1 %all-gather.18.cloned.1.call-done = bf16[3,1184,384]{2,1,0:T(8,128)(2,1)} async-done(((bf16[3,296,384]{2,1,0:T(8,128)(2,1)}), bf16[3,1184,384]{2,1,0:T(8,128)(2,1)}) %all-gather.18.cloned.1.call-update) | async-done | bytes 2727952 | tf_op jit(solution)/shard_map/all_gather | solution.py:122
  460.3 49.2 %all-gather.20.cloned.1.call-done = bf16[3,1184,384]{2,1,0:T(8,128)(2,1)} async-done(((bf16[3,296,384]{2,1,0:T(8,128)(2,1)}), bf16[3,1184,384]{2,1,0:T(8,128)(2,1)}) %all-gather.20.cloned.1.call-update) | async-done | bytes 2727952 | tf_op jit(solution)/shard_map/all_gather | solution.py:123
  518.5 53.4 %while.30 = (s32[]{:T(128)}, bf16[6,3,296,64]{2,3,1,0:T(8,128)(2,1)}, f32[6,3,296]{2,1,0:T(4,128)}, f32[6]{0:T(128)}, bf16[6,3,296,64]{2,3,1,0:T(8,128)(2,1)}, /...) while((s32[]{:T(128)}, ...), condition=%wide.region_12.13_spmd.clone, body=%wide.region_8.12_spmd.clone.sunk | while | flops 277630528 | bytes 13942453 | solution.py:149
  582.8 42.5 %reduce-scatter.8.cloned.1.call-done = f32[3,64,1536]{2,1,0:T(8,128)} async-done(((f32[3,256,1536]{2,1,0:T(8,128)}), f32[3,64,1536]{2,1,0:T(8,128)}) %reduce-scatter.8.cloned.1.call-update) | async-done | bytes 1179664 | tf_op jit(solution)/shard_map/reduce_scatter | solution.py:42
  637.4 127.8 %all-gather.28.cloned.1.call-done = bf16[2,1536,1536]{1,0,2:T(2,128)(2,1)} async-done(((bf16[2,1536,192]{1,0,2:T(2,128)(2,1)}), bf16[2,1536,1536]{1,0,2:T(2,128)(2,1)}) %all-gather.28.cloned.1.call-update) | async-done | bytes 9437200 | tf_op jit(solution)/shard_map/all_gather | solution.py:93
  765.2 19.1 fusion.191
  784.4 22.6 copy.359
  809.8 93.0 %all-gather.26.cloned.1.call-done = bf16[2,1536,1536]{2,1,0:T(8,128)(2,1)} async-done(((bf16[2,192,1536]{2,1,0:T(8,128)(2,1)}), bf16[2,1536,1536]{2,1,0:T(8,128)(2,1)}) %all-gather.26.cloned.1.call-update) | async-done | bytes 9437200 | tf_op jit(solution)/shard_map/all_gather | solution.py:92
  902.8 24.3 all-gather.24.cloned.1.call-done
  927.1 9.0 fusion.61
  936.1 17.2 all-gather.30.cloned.1.call-done
  953.3 9.5 fusion.49
  970.3 22.5 copy.364
  992.9 7.0 all_gather.66
  1001.6 7.2 all_gather.63
  1020.9 22.0 reduce-scatter.12.cloned.1.call-done
  1047.5 34.0 %all-reduce.26.cloned.1.call-done = f32[3,40,1536]{2,0,1:T(4,128)} async-done(((f32[3,40,1536]{2,0,1:T(4,128)}), f32[3,40,1536]{2,0,1:T(4,128)}) %all-reduce.26.cloned.1.call-update) | async-done | bytes 737296
  1092.9 15.0 all-gather.32.cloned.1.call-done
  1111.2 73.6 %while.31 = (s32[]{:T(128)}, f32[6,3,296,64]{2,3,1,0:T(8,128)}, bf16[6,3,1184,64]{2,3,1,0:T(8,128)(2,1)}, bf16[6,3,1184,64]{2,3,1,0:T(8,128)(2,1)}, bf16[6,3,296...) while((s32[]{:T(128)}, f32[6,3,296,64]{2,3,1,0:T(8,128)}, ...), condition=%wide.region_29.30_spmd.clone, body=%wide.region_27.29_spmd.clone.sunk | while | flops 681308224 | bytes 36244180 | solution.py:265
  1237.5 161.6 %all-reduce.36.cloned.1.call-done = (bf16[3,1184,384]{2,1,0:T(8,128)(2,1)}, bf16[3,1184,384]{2,1,0:T(8,128)(2,1)}) async-done(((bf16[3,1184,384]{2,1,0:T(8,128)(2,1)}, bf16[3,1184,384]{2,1,0:T(8,128)(2,1)}), (bf16[3,1184,384]{2,1,0:T(8,128)(2,1)}, bf16[3,1184,384]{2,1,0:T(8,128)(2,1)})) %all-reduce.36.cloned.1.call-update) | async-done | bytes 5455888
  1441.2 7.1 convolution_bitcast_fusion.9
  1448.5 10.1 fusion.56
  1466.1 10.4 convolution_bitcast_fusion.4
  1491.7 41.6 %reduce-scatter.14.cloned.1.call-done = f32[3,64,1536]{2,1,0:T(8,128)} async-done(((f32[3,256,1536]{2,1,0:T(8,128)}), f32[3,64,1536]{2,1,0:T(8,128)}) %reduce-scatter.14.cloned.1.call-update) | async-done | bytes 1179664 | tf_op jit(solution)/shard_map/reduce_scatter | solution.py:42
  1538.9 44.8 %reduce-scatter.10.cloned.1.call-done = f32[3,64,1536]{2,1,0:T(8,128)} async-done(((f32[3,256,1536]{2,1,0:T(8,128)}), f32[3,64,1536]{2,1,0:T(8,128)}) %reduce-scatter.10.cloned.1.call-update) | async-done | bytes 1179664 | tf_op jit(solution)/shard_map/reduce_scatter | solution.py:42
  1592.1 14.6 pad_maximum_fusion.1
  1606.7 28.4 copy.329
  1635.6 45.5 %all-reduce.22.cloned.1.call-done = bf16[2,3,6,1536]{3,1,0,2:T(4,128)(2,1)} async-done(((bf16[2,3,6,1536]{3,1,0,2:T(4,128)(2,1)}), bf16[2,3,6,1536]{3,1,0,2:T(4,128)(2,1)}) %all-reduce.22.cloned.1.call-update) | async-done | bytes 110608 | tf_op jit(solution)/shard_map/psum | solution.py:322
  1681.1 8.8 fusion.76
  1689.8 10.7 psum.22
  1703.3 8.1 copy.319
  1717.9 8.3 copy.325
  1735.4 13.3 pad_maximum_fusion.2
  1748.7 21.6 copy.322
  1777.2 6.7 pad_maximum_fusion
  1787.7 24.1 pmax.7
  1813.5 41.9 %psum.23 = f32[2,2,64]{2,1,0:T(2,128)} all-reduce(f32[2,2,64]{2,1,0:T(2,128)S(1)} %pad_maximum_fusion.13), channel_id=1, replica_groups=mesh['shard'=2,'ctx'=4,'tp'=4] {'shard','ctx','tp'}, use_global_device_ids=true, to_apply=%region_69.70 | all-reduce | flops 256 | bytes 2048 | tf_op jit(solution)/shard_map/psum | solution.py:325
  1855.4 399.6 %all-reduce.30.cloned.1.call-done = f32[2,1536,1536]{1,0,2:T(2,128)} async-done(((f32[2,1536,1536]{1,0,2:T(2,128)}), f32[2,1536,1536]{1,0,2:T(2,128)}) %all-reduce.30.cloned.1.call-update) | async-done | bytes 18874384
  2259.2 92.0 %all-reduce.28.cloned.1.call-done = bf16[2,384,6,384]{3,0,2,1:T(2,128)(2,1)} async-done(((bf16[2,384,6,384]{3,0,2,1:T(2,128)(2,1)}), bf16[2,384,6,384]{3,0,2,1:T(2,128)(2,1)}) %all-reduce.28.cloned.1.call-update) | async-done | bytes 3538960
  2356.1 566.9 %all-reduce.32.cloned.1.call-done = (f32[2,3,1536,384]{3,0,1,2:T(2,128)}, f32[2,384,1536]{1,0,2:T(2,128)}) async-done(((f32[2,3,1536,384]{3,0,1,2:T(2,128)}, f32[2,384,1536]{1,0,2:T(2,128)}), (f32[2,3,1536,384]{3,0,1,2:T(2,128)}, f32[2,384,1536]{1,0,2:T(2,128)})) %all-reduce.32.cloned.1.call-update) | async-done | bytes 18874384
  2928.5 307.5 %reduce-scatter.16.cloned.1.call-done = f32[2,192,1536]{2,1,0:T(8,128)} async-done(((f32[2,1536,1536]{2,1,0:T(8,128)}), f32[2,192,1536]{2,1,0:T(8,128)}) %reduce-scatter.16.cloned.1.call-update) | async-done | bytes 2359312 | tf_op jit(solution)/shard_map/reduce_scatter | solution.py:349
  (658 shorter events, 426.3 us)
Async XLA Ops:
  7.2 201.0 %copy-start.108 = (bf16[3,1536]{1,0:T(4,128)(2,1)S(1)}, bf16[3,1536]{1,0:T(4,128)(2,1)}, u32[]{:S(2)}) copy-start(bf16[3,1536]{1,0:T(4,128)(2,1)} %param.19) | copy-start | bytes 27652
  7.2 201.0 %all-gather.12.cloned.1.call-start = ((), (), s32[]{:S(2)}) async-start(), calls=%async_computation.5 | async-start | bytes 15925248 | tf_op jit(solution)/shard_map/all_gather | solution.py:98
  7.9 308.9 %all-gather.16.cloned.1.call-start = ((), (), s32[]{:S(2)}) async-start(), calls=%async_computation.7 | async-start | bytes 7962624 | tf_op jit(solution)/shard_map/all_gather | solution.py:90
  8.7 332.6 %all-gather.14.cloned.1.call-start = ((), (), s32[]{:S(2)}) async-start(), calls=%async_computation.6 | async-start | bytes 2949120 | tf_op jit(solution)/shard_map/all_gather | solution.py:35
  8.9 213.0 %copy-start.98 = (f32[3,64]{1,0:T(4,128)}, f32[3,64]{1,0:T(4,128)S(1)}, u32[]{:S(2)}) copy-start(f32[3,64]{1,0:T(4,128)S(1)} %broadcast_multiply_fusion.3) | copy-start | bytes 2308
  9.2 199.0 %copy-start.121 = (f32[3,64]{1,0:T(4,128)}, f32[3,64]{1,0:T(4,128)S(1)}, u32[]{:S(2)}) copy-start(f32[3,64]{1,0:T(4,128)S(1)} %fusion.97) | copy-start | bytes 2308
  9.2 212.6 %copy-start.117 = (f32[3,64]{1,0:T(4,128)}, f32[3,64]{1,0:T(4,128)S(1)}, u32[]{:S(2)}) copy-start(f32[3,64]{1,0:T(4,128)S(1)} %fusion.177) | copy-start | bytes 2308
  223.2 172.4 %all-gather.22.cloned.1.call-start = ((), (), s32[]{:S(2)}) async-start(), calls=%async_computation.10 | async-start | bytes 2654208 | tf_op jit(solution)/shard_map/all_gather | solution.py:91
  224.3 228.4 %all-gather.18.cloned.1.call-start = ((), (), s32[]{:S(2)}) async-start(), calls=%async_computation.8 | async-start | bytes 3409920 | tf_op jit(solution)/shard_map/all_gather | solution.py:122
  225.0 94.6 %copy-start.135 = (f32[64]{0:T(128)}, f32[64]{0:T(128)S(1)}, u32[]{:S(2)}) copy-start(f32[64]{0:T(128)S(1)} %get-tuple-element.454) | copy-start | bytes 772
  225.1 96.1 %copy-start.124 = (f32[384]{0:T(512)}, f32[384]{0:T(512)S(1)}, u32[]{:S(2)}) copy-start(f32[384]{0:T(512)S(1)} %mul.913) | copy-start | bytes 4612
  225.2 126.0 %copy-start.118 = (f32[384]{0:T(512)}, f32[384]{0:T(512)S(1)}, u32[]{:S(2)}) copy-start(f32[384]{0:T(512)S(1)} %mul.904) | copy-start | bytes 4612
  233.3 86.3 %copy-start.41 = (bf16[3,40,1536]{2,0,1:T(4,128)(2,1)}, bf16[3,40,1536]{2,0,1:T(4,128)(2,1)S(1)}, u32[]{:S(2)}) copy-start(bf16[3,40,1536]{2,0,1:T(4,128)(2,1)S(1)} %all_gather.56) | copy-start | bytes 1105924
  319.6 34.5 %copy-start.32 = (f32[3,3,40,384]{3,2,1,0:T(8,128)}, f32[3,3,40,384]{3,2,1,0:T(8,128)S(1)}, u32[]{:S(2)}) copy-start(f32[3,3,40,384]{3,2,1,0:T(8,128)S(1)} %fusion.93) | copy-start | bytes 1658884
  354.1 155.4 %all-gather.20.cloned.1.call-start = ((), (), s32[]{:S(2)}) async-start(), calls=%async_computation.9 | async-start | bytes 3409920 | tf_op jit(solution)/shard_map/all_gather | solution.py:123
  356.5 268.8 %reduce-scatter.8.cloned.1.call-start = ((), (), s32[]{:S(2)}) async-start(), calls=%async_computation.11 | async-start | bytes 5898240 | tf_op jit(solution)/shard_map/reduce_scatter | solution.py:42
  578.5 46.8 %copy-start.74 = (f32[3,1536]{1,0:T(4,128)S(1)}, f32[3,1536]{1,0:T(4,128)}, u32[]{:S(2)}) copy-start(f32[3,1536]{1,0:T(4,128)} %get-tuple-element.449) | copy-start | bytes 55300
  578.5 186.7 %all-gather.28.cloned.1.call-start = ((), (), s32[]{:S(2)}) async-start(), calls=%async_computation.14 | async-start | bytes 10616832 | tf_op jit(solution)/shard_map/all_gather | solution.py:93
  582.0 320.8 %all-gather.26.cloned.1.call-start = ((), (), s32[]{:S(2)}) async-start(), calls=%async_computation.13 | async-start | bytes 10616832 | tf_op jit(solution)/shard_map/all_gather | solution.py:92
  582.7 344.4 %all-gather.24.cloned.1.call-start = ((), (), s32[]{:S(2)}) async-start(), calls=%async_computation.12 | async-start | bytes 2949120 | tf_op jit(solution)/shard_map/all_gather | solution.py:35
  630.2 323.1 %all-gather.30.cloned.1.call-start = ((), (), s32[]{:S(2)}) async-start(), calls=%async_computation.16 | async-start | bytes 2949120 | tf_op jit(solution)/shard_map/all_gather | solution.py:35
  632.3 367.5 %all-reduce.24.cloned.1.call-start = ((), (), s32[]{:S(2)}) async-start(), calls=%async_computation.22 | async-start | bytes 1966080
  809.8 233.0 %reduce-scatter.12.cloned.1.call-start = ((), (), s32[]{:S(2)}) async-start(), calls=%async_computation.17 | async-start | bytes 5898240 | tf_op jit(solution)/shard_map/reduce_scatter | solution.py:42
  968.4 113.2 %all-reduce.26.cloned.1.call-start = ((), (), s32[]{:S(2)}) async-start(), calls=%async_computation.23 | async-start | bytes 1966080
  1001.2 82.3 %copy-start.12 = (f32[3,10,1536]{2,0,1:T(4,128)}, f32[3,10,1536]{2,0,1:T(4,128)S(1)}, u32[]{:S(2)}) copy-start(f32[3,10,1536]{2,0,1:T(4,128)S(1)} %get-tuple-element.409) | copy-start | bytes 552964
  1020.4 87.5 %all-gather.32.cloned.1.call-start = ((), (), s32[]{:S(2)}) async-start(), calls=%async_computation.18 | async-start | bytes 2949120 | tf_op jit(solution)/shard_map/all_gather | solution.py:35
  1045.8 35.8 %copy-start.61 = (f32[3,1536]{1,0:T(4,128)S(1)}, f32[3,1536]{1,0:T(4,128)}, u32[]{:S(2)}) copy-start(f32[3,1536]{1,0:T(4,128)} %get-tuple-element.440) | copy-start | bytes 55300
  1045.8 35.8 %copy-start.86 = (f32[3,10]{0,1:T(8,128)S(1)}, f32[3,10]{0,1:T(8,128)}, u32[]{:S(2)}) copy-start(f32[3,10]{0,1:T(8,128)} %copy-done.85) | copy-start | bytes 364
  1045.8 35.8 %copy-start.90 = (f32[3,10]{0,1:T(8,128)S(1)}, f32[3,10]{0,1:T(8,128)}, u32[]{:S(2)}) copy-start(f32[3,10]{0,1:T(8,128)} %copy-done.89) | copy-start | bytes 364
  1045.8 37.7 %copy-start.105 = (f32[3,10]{0,1:T(8,128)S(1)}, f32[3,10]{0,1:T(8,128)}, u32[]{:S(2)}) copy-start(f32[3,10]{0,1:T(8,128)} %copy-done.104) | copy-start | bytes 364
  1045.8 39.0 %copy-start.79 = (f32[3,1536]{1,0:T(4,128)S(1)}, f32[3,1536]{1,0:T(4,128)}, u32[]{:S(2)}) copy-start(f32[3,1536]{1,0:T(4,128)} %get-tuple-element.441) | copy-start | bytes 55300
  1045.8 37.7 %copy-start.126 = (f32[3,64]{1,0:T(4,128)}, f32[3,64]{1,0:T(4,128)S(1)}, u32[]{:S(2)}) copy-start(f32[3,64]{1,0:T(4,128)S(1)} %negate_multiply_fusion.3) | copy-start | bytes 2308
  1047.4 351.7 %all-reduce.36.cloned.1.call-start = ((), (), s32[]{:S(2)}) async-start(), calls=%async_computation.28 | async-start | bytes 10911744
  1203.0 280.0 %all-reduce.34.cloned.1.call-start = ((), (), s32[]{:S(2)}) async-start(), calls=%async_computation.27 | async-start | bytes 3932160
  1227.5 172.8 %copy-start.4 = (f32[3,256,384]{2,1,0:T(8,128)S(1)}, f32[3,256,384]{2,1,0:T(8,128)}, u32[]{:S(2)}) copy-start(f32[3,256,384]{2,1,0:T(8,128)} %copy-done.3) | copy-start | bytes 3538948
  1434.6 98.7 %reduce-scatter.14.cloned.1.call-start = ((), (), s32[]{:S(2)}) async-start(), calls=%async_computation.19 | async-start | bytes 5898240 | tf_op jit(solution)/shard_map/reduce_scatter | solution.py:42
  1448.3 135.4 %reduce-scatter.10.cloned.1.call-start = ((), (), s32[]{:S(2)}) async-start(), calls=%async_computation.15 | async-start | bytes 5898240 | tf_op jit(solution)/shard_map/reduce_scatter | solution.py:42
  1458.6 222.4 %all-reduce.22.cloned.1.call-start = ((), (), s32[]{:S(2)}) async-start(), calls=%async_computation.20 | async-start | bytes 294912 | tf_op jit(solution)/shard_map/psum | solution.py:322
  1476.5 56.8 %copy-start.2 = (bf16[3,64,1536]{2,1,0:T(8,128)(2,1)S(1)}, bf16[3,64,1536]{2,1,0:T(8,128)(2,1)}, u32[]{:S(2)}) copy-start(bf16[3,64,1536]{2,1,0:T(8,128)(2,1)} %param.17) | copy-start | bytes 1769476
  1476.5 56.8 %copy-start.99 = (f32[3,64]{1,0:T(4,128)S(1)}, f32[3,64]{1,0:T(4,128)}, u32[]{:S(2)}) copy-start(f32[3,64]{1,0:T(4,128)} %copy-done.98) | copy-start | bytes 2308
  1488.0 95.6 %copy-start.21 = (bf16[3,64,1536]{2,1,0:T(8,128)(2,1)S(1)}, bf16[3,64,1536]{2,1,0:T(8,128)(2,1)}, u32[]{:S(2)}) copy-start(bf16[3,64,1536]{2,1,0:T(8,128)(2,1)} %param.28) | copy-start | bytes 1769476
  1538.9 50.2 %copy-start.110 = (bf16[3,1536]{1,0:T(4,128)(2,1)S(1)}, bf16[3,1536]{1,0:T(4,128)(2,1)}, u32[]{:S(2)}) copy-start(bf16[3,1536]{1,0:T(4,128)(2,1)} %get-tuple-element.338) | copy-start | bytes 27652
  1592.1 662.9 %all-reduce.30.cloned.1.call-start = ((), (), s32[]{:S(2)}) async-start(), calls=%async_computation.25 | async-start | bytes 37748736
  1635.1 716.1 %all-reduce.28.cloned.1.call-start = ((), (), s32[]{:S(2)}) async-start(), calls=%async_computation.24 | async-start | bytes 7077888
  1635.6 64.9 %copy-start.109 = (bf16[3,1536]{1,0:T(4,128)(2,1)S(1)}, bf16[3,1536]{1,0:T(4,128)(2,1)}, u32[]{:S(2)}) copy-start(bf16[3,1536]{1,0:T(4,128)(2,1)} %param.19) | copy-start | bytes 27652
  1711.4 1211.6 %all-reduce.32.cloned.1.call-start = ((), (), s32[]{:S(2)}) async-start(), calls=%async_computation.26 | async-start | bytes 37748736
  1770.3 1465.7 %reduce-scatter.16.cloned.1.call-start = ((), (), s32[]{:S(2)}) async-start(), calls=%async_computation.21 | async-start | bytes 21233664 | tf_op jit(solution)/shard_map/reduce_scatter | solution.py:349
  1811.8 445.6 %copy-start.146 = (f32[6]{0:T(128)}, f32[6]{0:T(128)S(1)}, u32[]{:S(2)}) copy-start(f32[6]{0:T(128)S(1)} %pmax.7) | copy-start | bytes 76
  (128 other events, 1106.5 us)
Sparse Core Ops, SparseCore 0:
  10.1 197.9 all-gather.11
  210.3 106.4 all-gather.15
  319.0 22.2 all-gather.13
  343.8 51.8 all-gather.21
  397.6 55.0 all-gather.17
  454.2 55.2 all-gather.19
  578.6 46.5 reduce-scatter.7
  627.9 137.2 all-gather.27
  767.4 135.4 all-gather.25
  904.8 22.2 all-gather.23
  929.2 24.0 all-gather.29
  956.1 35.9 all-reduce.23
  994.7 48.0 reduce-scatter.11
  1045.6 35.8 all-reduce.25
  1083.5 24.3 all-gather.31
  1203.1 195.9 all-reduce.35
  1434.7 48.2 all-reduce.33
  1485.3 47.9 reduce-scatter.13
  1535.8 47.8 reduce-scatter.9
  1592.2 88.8 all-reduce.21
  1685.1 569.7 all-reduce.29
  2257.8 93.4 all-reduce.27
  2355.5 567.4 all-reduce.31
  2927.3 308.7 reduce-scatter.15
where the time goes:
time: 3260 us; the launch traced here: 3240 us
  waiting for transfers between devices  2470 us (76%)
  local copies, waits for them, and re-layouts  293 us (9%)
  matrix products  216 us (7%)
  other arithmetic  127 us (4%)
  blocking collectives  110 us (3%)
    unnamed x31, waiting for transfers between devices  1260 us
    reduce_scatter x1, waiting for transfers between devices, local(): lax.psum_scatter(grad_up, ('shard', 'ctx'), scatter_dimension=1, tiled=True)  308 us
    all_gather x1, waiting for transfers between devices, local(): mod_all = lax.all_gather(mod_w, ('shard', 'ctx'), axis=1, tiled=True)  199 us
    reduce_scatter x4, waiting for transfers between devices, reduce_rows(): lax.psum_scatter(first, 'tp', scatter_dimension=1, tiled=True)  151 us
    all_gather x1, waiting for transfers between devices, local(): lax.all_gather(down_w, ('shard', 'ctx'), axis=2, tiled=True)  128 us
    unnamed x337, local copies, waits for them, and re-layouts  106 us
    all_gather x1, waiting for transfers between devices, local(): lax.all_gather(up_w, ('shard', 'ctx'), axis=1, tiled=True)  93 us
    all_gather x1, waiting for transfers between devices, local(): lax.all_gather(qkv_w, ('shard', 'ctx'), axis=2, tiled=True)  83.5 us
  transfers between devices with their start and end apart: 24, of which 23 were waited for; matrix products, arithmetic and copies ran while one was open for 13% of the time, Pallas kernels for 0%

commit v1 on v0

--- a/solution.py
+++ b/solution.py
@@ -5,6 +5,27 @@
 
 EPS = 1e-06
 QUERY_SCALE = 0.125
+
+
+def gather_around(x, axis, dim):
+    length, position, rows = (lax.axis_size(axis), lax.axis_index(axis), x.shape[dim])
+    right = [(i, (i + 1) % length) for i in range(length)]
+    left = [(i, (i - 1) % length) for i in range(length)]
+    result = jnp.zeros((*x.shape[:dim], length * rows, *x.shape[dim + 1 :]), x.dtype)
+    result = lax.dynamic_update_slice_in_dim(result, x, position * rows, axis=dim)
+    from_left = from_right = x
+    half = length // 2
+    for step in range(1, half + 1):
+        from_left = lax.ppermute(from_left, axis, right)
+        result = lax.dynamic_update_slice_in_dim(
+            result, from_left, (position - step) % length * rows, axis=dim
+        )
+        if step < length - half:
+            from_right = lax.ppermute(from_right, axis, left)
+            result = lax.dynamic_update_slice_in_dim(
+                result, from_right, (position + step) % length * rows, axis=dim
+            )
+    return result
 
 
 def layer_norm(values):
@@ -90,7 +111,7 @@
         lax.all_gather(qkv_w, ("shard", "ctx"), axis=2, tiled=True),
         lax.all_gather(o_w, ("shard", "ctx"), axis=2, tiled=True),
         lax.all_gather(up_w, ("shard", "ctx"), axis=1, tiled=True),
-        lax.all_gather(down_w, ("shard", "ctx"), axis=2, tiled=True),
+        gather_around(down_w, ("shard", "ctx"), 2),
     )
     qkv_all, out_all, up_all, down_all = gathered
     cond_float = cond.astype(jnp.float32)

time: 3260 us -> 3450 us (1.058)
  local copies, waits for them, and re-layouts: 293 us -> 448 us
    ppermute x0 -> x7, waiting for transfers between devices: none -> 188 us  [the longest x3 160 us: gather_around(): from_right = lax.ppermute(from_right, axis, left)]
    unnamed x31, waiting for transfers between devices: 1260 us -> 1100 us
    dynamic_update_slice x0 -> x8, local copies, waits for them, and re-layouts: none -> 131 us  [the longest x4 64.9 us: gather_around(): lax.dynamic_update_slice_in_dim(result, from_left, (position - step) % le...]
    unnamed x337 -> x348, local copies, waits for them, and re-layouts: 106 us -> 108 us
  transfers between devices with their start and end apart: 24 -> 31, of which waited for: 23 -> 26; matrix products, arithmetic and copies ran while one was open for 13% -> 19% of each run, Pallas kernels for 0% -> 0%
where the time goes in v1:
time: 3450 us; the launch traced here: 3430 us
  waiting for transfers between devices  2500 us (72%)
  local copies, waits for them, and re-layouts  448 us (13%)
  matrix products  216 us (6%)
  other arithmetic  127 us (4%)
  blocking collectives  110 us (3%)
    unnamed x31, waiting for transfers between devices  1100 us
    reduce_scatter x1, waiting for transfers between devices, local(): lax.psum_scatter(grad_up, ('shard', 'ctx'), scatter_dimension=1, tiled=True)  308 us
    all_gather x1, waiting for transfers between devices, local(): mod_all = lax.all_gather(mod_w, ('shard', 'ctx'), axis=1, tiled=True)  199 us
    ppermute x3, waiting for transfers between devices, gather_around(): from_right = lax.ppermute(from_right, axis, left)  160 us
    reduce_scatter x4, waiting for transfers between devices, reduce_rows(): lax.psum_scatter(first, 'tp', scatter_dimension=1, tiled=True)  151 us
    all_gather x1, waiting for transfers between devices, local(): lax.all_gather(down_w, ('shard', 'ctx'), axis=2, tiled=True)  128 us
    unnamed x348, local copies, waits for them, and re-layouts  108 us
    all_gather x1, waiting for transfers between devices, local(): lax.all_gather(up_w, ('shard', 'ctx'), axis=1, tiled=True)  92.6 us
  transfers between devices with their start and end apart: 31, of which 26 were waited for; matrix products, arithmetic and copies ran while one was open for 19% of the time, Pallas kernels for 0%

profile of v1, /device:TPU:0, one launch (start us, length us, event | category | flops | bytes accessed | tf_op | source)
XLA Modules:
  0.0 3431.2 jit_solution(982269765275253775)
XLA Ops:
  9.2 199.0 %all-gather.12.cloned.1.call-done = bf16[2,1536,6,384]{3,1,2,0:T(8,128)(2,1)} async-done(((bf16[2,192,6,384]{3,1,2,0:T(8,128)(2,1)}), bf16[2,1536,6,384]{3,1,2,0:T(8,128)(2,1)}) %all-gather.12.cloned.1.call-update) | async-done | bytes 14155792 | tf_op jit(solution)/shard_map/all_gather | solution.py:119
  233.7 83.2 %all-gather.16.cloned.1.call-done = bf16[2,3,1536,384]{3,2,1,0:T(8,128)(2,1)} async-done(((bf16[2,3,192,384]{3,2,1,0:T(8,128)(2,1)}), bf16[2,3,1536,384]{3,2,1,0:T(8,128)(2,1)}) %all-gather.16.cloned.1.call-update) | async-done | bytes 7077904 | tf_op jit(solution)/shard_map/all_gather | solution.py:111
  321.9 19.3 all-gather.14.cloned.1.call-done
  356.7 38.9 %all-gather.22.cloned.1.call-done = bf16[2,384,1536]{1,0,2:T(2,128)(2,1)} async-done(((bf16[2,384,192]{1,0,2:T(2,128)(2,1)}), bf16[2,384,1536]{1,0,2:T(2,128)(2,1)}) %all-gather.22.cloned.1.call-update) | async-done | bytes 2359312 | tf_op jit(solution)/shard_map/all_gather | solution.py:112
  412.7 40.0 %all-gather.18.cloned.1.call-done = bf16[3,1184,384]{2,1,0:T(8,128)(2,1)} async-done(((bf16[3,296,384]{2,1,0:T(8,128)(2,1)}), bf16[3,1184,384]{2,1,0:T(8,128)(2,1)}) %all-gather.18.cloned.1.call-update) | async-done | bytes 2727952 | tf_op jit(solution)/shard_map/all_gather | solution.py:143
  460.3 49.1 %all-gather.20.cloned.1.call-done = bf16[3,1184,384]{2,1,0:T(8,128)(2,1)} async-done(((bf16[3,296,384]{2,1,0:T(8,128)(2,1)}), bf16[3,1184,384]{2,1,0:T(8,128)(2,1)}) %all-gather.20.cloned.1.call-update) | async-done | bytes 2727952 | tf_op jit(solution)/shard_map/all_gather | solution.py:144
  518.6 53.4 %while.30 = (s32[]{:T(128)}, bf16[6,3,296,64]{2,3,1,0:T(8,128)(2,1)}, f32[6,3,296]{2,1,0:T(4,128)}, f32[6]{0:T(128)}, bf16[6,3,296,64]{2,3,1,0:T(8,128)(2,1)}, /...) while((s32[]{:T(128)}, ...), condition=%wide.region_12.13_spmd.clone, body=%wide.region_8.12_spmd.clone.sunk | while | flops 277630528 | bytes 13942953 | solution.py:170
  582.9 42.4 %reduce-scatter.8.cloned.1.call-done = f32[3,64,1536]{2,1,0:T(8,128)} async-done(((f32[3,256,1536]{2,1,0:T(8,128)}), f32[3,64,1536]{2,1,0:T(8,128)}) %reduce-scatter.8.cloned.1.call-update) | async-done | bytes 1179664 | tf_op jit(solution)/shard_map/reduce_scatter | solution.py:63
  637.7 127.6 %all-gather.30.cloned.1.call-done = bf16[2,1536,1536]{1,0,2:T(2,128)(2,1)} async-done(((bf16[2,1536,192]{1,0,2:T(2,128)(2,1)}), bf16[2,1536,1536]{1,0,2:T(2,128)(2,1)}) %all-gather.30.cloned.1.call-update) | async-done | bytes 9437200 | tf_op jit(solution)/shard_map/all_gather | solution.py:197
  765.3 19.5 fusion.189
  784.9 22.6 copy.389
  810.3 92.6 %all-gather.26.cloned.1.call-done = bf16[2,1536,1536]{2,1,0:T(8,128)(2,1)} async-done(((bf16[2,192,1536]{2,1,0:T(8,128)(2,1)}), bf16[2,1536,1536]{2,1,0:T(8,128)(2,1)}) %all-gather.26.cloned.1.call-update) | async-done | bytes 9437200 | tf_op jit(solution)/shard_map/all_gather | solution.py:113
  902.9 24.3 all-gather.24.cloned.1.call-done
  936.1 17.3 all-gather.28.cloned.1.call-done
  953.4 9.4 fusion.49
  970.4 22.5 copy.394
  1020.8 22.4 reduce-scatter.12.cloned.1.call-done
  1049.3 32.8 all-reduce.26.cloned.1.call-done
  1093.5 14.7 all-gather.32.cloned.1.call-done
  1111.5 73.7 %while.31 = (s32[]{:T(128)}, f32[6,3,296,64]{2,3,1,0:T(8,128)}, bf16[6,3,1184,64]{2,3,1,0:T(8,128)(2,1)}, bf16[6,3,1184,64]{2,3,1,0:T(8,128)(2,1)}, bf16[6,3,296...) while((s32[]{:T(128)}, f32[6,3,296,64]{2,3,1,0:T(8,128)}, ...), condition=%wide.region_29.30_spmd.clone, body=%wide.region_27.29_spmd.clone.sunk | while | flops 681308224 | bytes 36244172 | solution.py:286
  1208.9 88.5 %collective-permute-done.1 = bf16[2,1536,192]{1,2,0:T(8,128)(2,1)S(1)} collective-permute-done((bf16[2,1536,192]{1,2,0:T(8,128)(2,1)S(1)}, bf16[2,1536,192]{1,2,0:T(8,128)(2,1)S(1)}, u32[]{:S(2)}, u32[]{:S(2)}) %collective-permute-start.1) | collective-permute-done | bytes 1179680 | tf_op jit(solution)/shard_map/ppermute | solution.py:24
  1298.4 12.7 collective-permute-done.2
  1313.5 71.6 %collective-permute-done.3 = bf16[2,1536,192]{1,2,0:T(8,128)(2,1)} collective-permute-done((bf16[2,1536,192]{1,2,0:T(8,128)(2,1)S(1)}, bf16[2,1536,192]{1,2,0:T(8,128)(2,1)}, u32[]{:S(2)}, u32[]{:S(2)}) %collective-permute-start.3) | collective-permute-done | bytes 1179680 | tf_op jit(solution)/shard_map/ppermute | solution.py:24
  1385.1 14.8 collective-permute-done.4
  1408.5 15.4 dynamic_update_slice.47
  1426.5 16.7 dynamic_update_slice.48
  1444.7 17.5 dynamic_update_slice.49
  1463.8 15.2 dynamic_update_slice.50
  1481.5 15.4 dynamic_update_slice.51
  1499.4 17.5 dynamic_update_slice.52
  1519.4 17.4 dynamic_update_slice.53
  1539.3 15.5 dynamic_update_slice.54
  1636.0 10.1 fusion.51
  1653.6 10.5 convolution_bitcast_fusion.4
  1679.9 41.6 %reduce-scatter.14.cloned.1.call-done = f32[3,64,1536]{2,1,0:T(8,128)} async-done(((f32[3,256,1536]{2,1,0:T(8,128)}), f32[3,64,1536]{2,1,0:T(8,128)}) %reduce-scatter.14.cloned.1.call-update) | async-done | bytes 1179664 | tf_op jit(solution)/shard_map/reduce_scatter | solution.py:63
  1727.1 44.8 %reduce-scatter.10.cloned.1.call-done = f32[3,64,1536]{2,1,0:T(8,128)} async-done(((f32[3,256,1536]{2,1,0:T(8,128)}), f32[3,64,1536]{2,1,0:T(8,128)}) %reduce-scatter.10.cloned.1.call-update) | async-done | bytes 1179664 | tf_op jit(solution)/shard_map/reduce_scatter | solution.py:63
  1780.3 14.6 pad_maximum_fusion.1
  1794.9 28.4 copy.359
  1823.6 45.6 %all-reduce.22.cloned.1.call-done = bf16[2,3,6,1536]{3,1,0,2:T(4,128)(2,1)} async-done(((bf16[2,3,6,1536]{3,1,0,2:T(4,128)(2,1)}), bf16[2,3,6,1536]{3,1,0,2:T(4,128)(2,1)}) %all-reduce.22.cloned.1.call-update) | async-done | bytes 110608 | tf_op jit(solution)/shard_map/psum | solution.py:343
  1878.0 10.7 psum.22
  1923.6 13.3 pad_maximum_fusion.2
  1936.9 21.6 copy.352
  1975.9 24.1 pmax.7
  2001.7 41.9 %psum.23 = f32[2,2,64]{2,1,0:T(2,128)} all-reduce(f32[2,2,64]{2,1,0:T(2,128)S(1)} %pad_maximum_fusion.13), channel_id=1, replica_groups=mesh['shard'=2,'ctx'=4,'tp'=4] {'shard','ctx','tp'}, use_global_device_ids=true, to_apply=%region_69.70 | all-reduce | flops 256 | bytes 2048 | tf_op jit(solution)/shard_map/psum | solution.py:346
  2043.6 399.4 %all-reduce.30.cloned.1.call-done = f32[2,1536,1536]{1,0,2:T(2,128)} async-done(((f32[2,1536,1536]{1,0,2:T(2,128)}), f32[2,1536,1536]{1,0,2:T(2,128)}) %all-reduce.30.cloned.1.call-update) | async-done | bytes 18874384
  2447.3 92.0 %all-reduce.28.cloned.1.call-done = bf16[2,384,6,384]{3,0,2,1:T(2,128)(2,1)} async-done(((bf16[2,384,6,384]{3,0,2,1:T(2,128)(2,1)}), bf16[2,384,6,384]{3,0,2,1:T(2,128)(2,1)}) %all-reduce.28.cloned.1.call-update) | async-done | bytes 3538960
  2544.1 566.9 %all-reduce.32.cloned.1.call-done = (f32[2,3,1536,384]{3,0,1,2:T(2,128)}, f32[2,384,1536]{1,0,2:T(2,128)}) async-done(((f32[2,3,1536,384]{3,0,1,2:T(2,128)}, f32[2,384,1536]{1,0,2:T(2,128)}), (f32[2,3,1536,384]{3,0,1,2:T(2,128)}, f32[2,384,1536]{1,0,2:T(2,128)})) %all-reduce.32.cloned.1.call-update) | async-done | bytes 18874384
  3116.6 307.5 %reduce-scatter.16.cloned.1.call-done = f32[2,192,1536]{2,1,0:T(8,128)} async-done(((f32[2,1536,1536]{2,1,0:T(8,128)}), f32[2,192,1536]{2,1,0:T(8,128)}) %reduce-scatter.16.cloned.1.call-update) | async-done | bytes 2359312 | tf_op jit(solution)/shard_map/reduce_scatter | solution.py:370
  (699 shorter events, 542.6 us)
Async XLA Ops:
  7.2 201.0 %copy-start.112 = (bf16[3,1536]{1,0:T(4,128)(2,1)S(1)}, bf16[3,1536]{1,0:T(4,128)(2,1)}, u32[]{:S(2)}) copy-start(bf16[3,1536]{1,0:T(4,128)(2,1)} %param.19) | copy-start | bytes 27652
  7.2 201.0 %all-gather.12.cloned.1.call-start = ((), (), s32[]{:S(2)}) async-start(), calls=%async_computation.5 | async-start | bytes 15925248 | tf_op jit(solution)/shard_map/all_gather | solution.py:119
  7.9 308.9 %all-gather.16.cloned.1.call-start = ((), (), s32[]{:S(2)}) async-start(), calls=%async_computation.7 | async-start | bytes 7962624 | tf_op jit(solution)/shard_map/all_gather | solution.py:111
  8.7 332.6 %all-gather.14.cloned.1.call-start = ((), (), s32[]{:S(2)}) async-start(), calls=%async_computation.6 | async-start | bytes 2949120 | tf_op jit(solution)/shard_map/all_gather | solution.py:56
  8.9 213.0 %copy-start.102 = (f32[3,64]{1,0:T(4,128)}, f32[3,64]{1,0:T(4,128)S(1)}, u32[]{:S(2)}) copy-start(f32[3,64]{1,0:T(4,128)S(1)} %broadcast_multiply_fusion.3) | copy-start | bytes 2308
  9.2 199.0 %copy-start.125 = (f32[3,64]{1,0:T(4,128)}, f32[3,64]{1,0:T(4,128)S(1)}, u32[]{:S(2)}) copy-start(f32[3,64]{1,0:T(4,128)S(1)} %fusion.95) | copy-start | bytes 2308
  9.2 212.6 %copy-start.121 = (f32[3,64]{1,0:T(4,128)}, f32[3,64]{1,0:T(4,128)S(1)}, u32[]{:S(2)}) copy-start(f32[3,64]{1,0:T(4,128)S(1)} %fusion.175) | copy-start | bytes 2308
  223.2 172.4 %all-gather.22.cloned.1.call-start = ((), (), s32[]{:S(2)}) async-start(), calls=%async_computation.10 | async-start | bytes 2654208 | tf_op jit(solution)/shard_map/all_gather | solution.py:112
  224.3 228.4 %all-gather.18.cloned.1.call-start = ((), (), s32[]{:S(2)}) async-start(), calls=%async_computation.8 | async-start | bytes 3409920 | tf_op jit(solution)/shard_map/all_gather | solution.py:143
  225.5 125.7 %copy-start.122 = (f32[384]{0:T(512)}, f32[384]{0:T(512)S(1)}, u32[]{:S(2)}) copy-start(f32[384]{0:T(512)S(1)} %mul.931) | copy-start | bytes 4612
  225.5 95.7 %copy-start.128 = (f32[384]{0:T(512)}, f32[384]{0:T(512)S(1)}, u32[]{:S(2)}) copy-start(f32[384]{0:T(512)S(1)} %mul.940) | copy-start | bytes 4612
  233.7 85.9 %copy-start.42 = (bf16[3,40,1536]{2,0,1:T(4,128)(2,1)}, bf16[3,40,1536]{2,0,1:T(4,128)(2,1)S(1)}, u32[]{:S(2)}) copy-start(bf16[3,40,1536]{2,0,1:T(4,128)(2,1)S(1)} %all_gather.55) | copy-start | bytes 1105924
  354.1 155.4 %all-gather.20.cloned.1.call-start = ((), (), s32[]{:S(2)}) async-start(), calls=%async_computation.9 | async-start | bytes 3409920 | tf_op jit(solution)/shard_map/all_gather | solution.py:144
  356.4 268.9 %reduce-scatter.8.cloned.1.call-start = ((), (), s32[]{:S(2)}) async-start(), calls=%async_computation.11 | async-start | bytes 5898240 | tf_op jit(solution)/shard_map/reduce_scatter | solution.py:63
  578.6 186.7 %all-gather.30.cloned.1.call-start = ((), (), s32[]{:S(2)}) async-start(), calls=%async_computation.16 | async-start | bytes 10616832 | tf_op jit(solution)/shard_map/all_gather | solution.py:197
  582.1 320.8 %all-gather.26.cloned.1.call-start = ((), (), s32[]{:S(2)}) async-start(), calls=%async_computation.13 | async-start | bytes 10616832 | tf_op jit(solution)/shard_map/all_gather | solution.py:113
  582.8 344.3 %all-gather.24.cloned.1.call-start = ((), (), s32[]{:S(2)}) async-start(), calls=%async_computation.12 | async-start | bytes 2949120 | tf_op jit(solution)/shard_map/all_gather | solution.py:56
  630.3 323.1 %all-gather.28.cloned.1.call-start = ((), (), s32[]{:S(2)}) async-start(), calls=%async_computation.15 | async-start | bytes 2949120 | tf_op jit(solution)/shard_map/all_gather | solution.py:56
  632.4 367.6 %all-reduce.24.cloned.1.call-start = ((), (), s32[]{:S(2)}) async-start(), calls=%async_computation.22 | async-start | bytes 1966080
  810.3 232.9 %reduce-scatter.12.cloned.1.call-start = ((), (), s32[]{:S(2)}) async-start(), calls=%async_computation.17 | async-start | bytes 5898240 | tf_op jit(solution)/shard_map/reduce_scatter | solution.py:63
  968.5 113.7 %all-reduce.26.cloned.1.call-start = ((), (), s32[]{:S(2)}) async-start(), calls=%async_computation.23 | async-start | bytes 1966080
  1001.4 82.7 %copy-start.12 = (f32[3,10,1536]{2,0,1:T(4,128)}, f32[3,10,1536]{2,0,1:T(4,128)S(1)}, u32[]{:S(2)}) copy-start(f32[3,10,1536]{2,0,1:T(4,128)S(1)} %get-tuple-element.409) | copy-start | bytes 552964
  1020.5 87.7 %all-gather.32.cloned.1.call-start = ((), (), s32[]{:S(2)}) async-start(), calls=%async_computation.18 | async-start | bytes 2949120 | tf_op jit(solution)/shard_map/all_gather | solution.py:56
  1047.7 538.8 %all-reduce.36.cloned.1.call-start = ((), (), s32[]{:S(2)}) async-start(), calls=%async_computation.28 | async-start | bytes 10911744
  1047.8 161.1 %collective-permute-start = (bf16[2,1536,192]{1,2,0:T(8,128)(2,1)}, bf16[2,1536,192]{1,2,0:T(8,128)(2,1)}, u32[]{:S(2)}, u32[]{:S(2)}) collective-permute-start(bf16[2,1536,192]{1,2,0:T(8,128)(2,1)} %param.25), channel_id=1, source_target_pairs={{0,4},{4,8},{8,12},{12,16},{16,20},{20,24},{24,28},{28,0},{1,5},{5... | collective-permute-start | bytes 3538952 | tf_op jit(solution)/shard_map/ppermute | solution.py:19
  1203.4 198.7 %copy-start.149 = (u32[32]{0:T(128)S(1)}, u32[32]{0:T(128)}, u32[]{:S(2)}) copy-start(u32[32]{0:T(128)} %constant.233) | copy-start | bytes 388
  1203.4 199.3 %copy-start.139 = (f32[2,2,64]{2,1,0:T(2,128)S(1)}, f32[2,2,64]{2,1,0:T(2,128)}, u32[]{:S(2)}) copy-start(f32[2,2,64]{2,1,0:T(2,128)} %param.26) | copy-start | bytes 3076
  1203.4 467.7 %all-reduce.34.cloned.1.call-start = ((), (), s32[]{:S(2)}) async-start(), calls=%async_computation.27 | async-start | bytes 3932160
  1204.7 92.8 %collective-permute-start.1 = (bf16[2,1536,192]{1,2,0:T(8,128)(2,1)S(1)}, bf16[2,1536,192]{1,2,0:T(8,128)(2,1)S(1)}, u32[]{:S(2)}, u32[]{:S(2)}) collective-permute-start(bf16[2,1536,192]{1,2,0:T(8,128)(2,1)S(1)} %copy-done.27), channel_id=1, source_target_pairs={{0,28},{4,0},{8,4},{12,8},{16,12},{20,16},{24,20},{28,24},{1,29},{... | collective-permute-start | bytes 3538952 | tf_op jit(solution)/shard_map/ppermute | solution.py:24
  1208.9 102.2 %collective-permute-start.2 = (bf16[2,1536,192]{1,2,0:T(8,128)(2,1)}, bf16[2,1536,192]{1,2,0:T(8,128)(2,1)S(1)}, u32[]{:S(2)}, u32[]{:S(2)}) collective-permute-start(bf16[2,1536,192]{1,2,0:T(8,128)(2,1)} %collective-permute-done), channel_id=1, source_target_pairs={{0,4},{4,8},{8,12},{12,16},{16,20},{20,24},{24,28},{28,0},{1,5},{5... | collective-permute-start | bytes 3538952 | tf_op jit(solution)/shard_map/ppermute | solution.py:19
  1298.4 86.7 %collective-permute-start.3 = (bf16[2,1536,192]{1,2,0:T(8,128)(2,1)S(1)}, bf16[2,1536,192]{1,2,0:T(8,128)(2,1)}, u32[]{:S(2)}, u32[]{:S(2)}) collective-permute-start(bf16[2,1536,192]{1,2,0:T(8,128)(2,1)S(1)} %collective-permute-done.1), channel_id=1, source_target_pairs={{0,28},{4,0},{8,4},{12,8},{16,12},{20,16},{24,20},{28,24},{1,29},{... | collective-permute-start | bytes 3538952 | tf_op jit(solution)/shard_map/ppermute | solution.py:24
  1311.1 74.0 %copy-start.49 = (bf16[2,1536,192]{1,2,0:T(8,128)(2,1)}, bf16[2,1536,192]{1,2,0:T(8,128)(2,1)S(1)}, u32[]{:S(2)}) copy-start(bf16[2,1536,192]{1,2,0:T(8,128)(2,1)S(1)} %collective-permute-done.2) | copy-start | bytes 3538948
  1311.1 88.8 %collective-permute-start.4 = (bf16[2,1536,192]{1,2,0:T(8,128)(2,1)S(1)}, bf16[2,1536,192]{1,2,0:T(8,128)(2,1)}, u32[]{:S(2)}, u32[]{:S(2)}) collective-permute-start(bf16[2,1536,192]{1,2,0:T(8,128)(2,1)S(1)} %collective-permute-done.2), channel_id=1, source_target_pairs={{0,4},{4,8},{8,12},{12,16},{16,20},{20,24},{24,28},{28,0},{1,5},{5... | collective-permute-start | bytes 3538952 | tf_op jit(solution)/shard_map/ppermute | solution.py:19
  1385.1 131.8 %collective-permute-start.5 = (bf16[2,1536,192]{1,2,0:T(8,128)(2,1)}, bf16[2,1536,192]{1,2,0:T(8,128)(2,1)}, u32[]{:S(2)}, u32[]{:S(2)}) collective-permute-start(bf16[2,1536,192]{1,2,0:T(8,128)(2,1)} %collective-permute-done.3), channel_id=1, source_target_pairs={{0,28},{4,0},{8,4},{12,8},{16,12},{20,16},{24,20},{28,24},{1,29},{... | collective-permute-start | bytes 3538952 | tf_op jit(solution)/shard_map/ppermute | solution.py:24
  1399.9 136.8 %collective-permute-start.6 = (bf16[2,1536,192]{1,2,0:T(8,128)(2,1)}, bf16[2,1536,192]{1,2,0:T(8,128)(2,1)}, u32[]{:S(2)}, u32[]{:S(2)}) collective-permute-start(bf16[2,1536,192]{1,2,0:T(8,128)(2,1)} %collective-permute-done.4), channel_id=1, source_target_pairs={{0,4},{4,8},{8,12},{12,16},{16,20},{20,24},{24,28},{28,0},{1,5},{5... | collective-permute-start | bytes 3538952 | tf_op jit(solution)/shard_map/ppermute | solution.py:19
  1621.9 99.6 %reduce-scatter.14.cloned.1.call-start = ((), (), s32[]{:S(2)}) async-start(), calls=%async_computation.19 | async-start | bytes 5898240 | tf_op jit(solution)/shard_map/reduce_scatter | solution.py:63
  1635.6 136.3 %reduce-scatter.10.cloned.1.call-start = ((), (), s32[]{:S(2)}) async-start(), calls=%async_computation.14 | async-start | bytes 5898240 | tf_op jit(solution)/shard_map/reduce_scatter | solution.py:63
  1646.1 223.1 %all-reduce.22.cloned.1.call-start = ((), (), s32[]{:S(2)}) async-start(), calls=%async_computation.20 | async-start | bytes 294912 | tf_op jit(solution)/shard_map/psum | solution.py:343
  1664.1 57.4 %copy-start.2 = (bf16[3,64,1536]{2,1,0:T(8,128)(2,1)S(1)}, bf16[3,64,1536]{2,1,0:T(8,128)(2,1)}, u32[]{:S(2)}) copy-start(bf16[3,64,1536]{2,1,0:T(8,128)(2,1)} %param.17) | copy-start | bytes 1769476
  1664.1 57.4 %copy-start.103 = (f32[3,64]{1,0:T(4,128)S(1)}, f32[3,64]{1,0:T(4,128)}, u32[]{:S(2)}) copy-start(f32[3,64]{1,0:T(4,128)} %copy-done.102) | copy-start | bytes 2308
  1676.2 95.7 %copy-start.21 = (bf16[3,64,1536]{2,1,0:T(8,128)(2,1)S(1)}, bf16[3,64,1536]{2,1,0:T(8,128)(2,1)}, u32[]{:S(2)}) copy-start(bf16[3,64,1536]{2,1,0:T(8,128)(2,1)} %param.28) | copy-start | bytes 1769476
  1727.1 50.3 %copy-start.114 = (bf16[3,1536]{1,0:T(4,128)(2,1)S(1)}, bf16[3,1536]{1,0:T(4,128)(2,1)}, u32[]{:S(2)}) copy-start(bf16[3,1536]{1,0:T(4,128)(2,1)} %get-tuple-element.338) | copy-start | bytes 27652
  1780.3 662.7 %all-reduce.30.cloned.1.call-start = ((), (), s32[]{:S(2)}) async-start(), calls=%async_computation.25 | async-start | bytes 37748736
  1823.4 716.0 %all-reduce.28.cloned.1.call-start = ((), (), s32[]{:S(2)}) async-start(), calls=%async_computation.24 | async-start | bytes 7077888
  1823.6 65.1 %copy-start.113 = (bf16[3,1536]{1,0:T(4,128)(2,1)S(1)}, bf16[3,1536]{1,0:T(4,128)(2,1)}, u32[]{:S(2)}) copy-start(bf16[3,1536]{1,0:T(4,128)(2,1)} %param.19) | copy-start | bytes 27652
  1899.6 1211.5 %all-reduce.32.cloned.1.call-start = ((), (), s32[]{:S(2)}) async-start(), calls=%async_computation.26 | async-start | bytes 37748736
  1958.5 1465.6 %reduce-scatter.16.cloned.1.call-start = ((), (), s32[]{:S(2)}) async-start(), calls=%async_computation.21 | async-start | bytes 21233664 | tf_op jit(solution)/shard_map/reduce_scatter | solution.py:370
  2000.0 445.5 %copy-start.151 = (f32[6]{0:T(128)}, f32[6]{0:T(128)S(1)}, u32[]{:S(2)}) copy-start(f32[6]{0:T(128)S(1)} %pmax.7) | copy-start | bytes 76
  (140 other events, 1484.5 us)
Sparse Core Ops, SparseCore 0:
  10.1 197.9 all-gather.11
  210.3 106.4 all-gather.15
  319.0 22.2 all-gather.13
  343.8 51.8 all-gather.21
  397.6 55.0 all-gather.17
  454.2 55.2 all-gather.19
  578.7 46.5 reduce-scatter.7
  628.0 137.2 all-gather.29
  767.4 135.4 all-gather.25
  904.9 22.2 all-gather.23
  929.3 24.0 all-gather.27
  956.2 35.8 all-reduce.23
  994.7 48.4 reduce-scatter.11
  1046.0 36.1 all-reduce.25
  1084.1 24.0 all-gather.31
  1203.5 333.5 all-reduce.35
  1622.0 49.0 all-reduce.33
  1673.5 47.9 reduce-scatter.13
  1724.0 47.8 reduce-scatter.9
  1780.4 88.7 all-reduce.21
  1873.3 569.6 all-reduce.29
  2445.9 93.4 all-reduce.27
  2543.6 567.4 all-reduce.31
  3115.4 308.7 reduce-scatter.15
